TPU v7x, 128 devices: a whole 4x4x4 slice. The times are simulated.
128 devices in a mesh: gx: 8 (over z, core), gy: 16 (over y, x).
Axes of the slice: x: 4, y: 4, z: 4, core: 2. Of those that a mesh axis runs over, the one named last changes fastest.
Arguments:
- panels: float32 [3, 1024, 2048], P(None, 'gy', 'gx'), may hold values from -4 to 4
- regrid_tiles: float32 [16, 256, 512], replicated, may hold values from -0.375 to 0.375
- weight_index: int32 [8, 2048, 2], P('gx', 'gy'), may hold values from 0 to 15
- owner: int32 [8, 2048, 1], P('gx', 'gy'), may hold values from 0 to 127; in each aligned block of 128 rows (0 to 127, 128 to 255, ..., all dimensions but the last counted through in order) at most 2 rows name the same one
- surface_type: int32 [2048, 4096], P('gy', 'gx'), may hold values from 0 to 3
- substrate: float32 [8, 2048, 4096], P(None, 'gy', 'gx'), may hold values from 0.5 to 1.5
- conductivity: float32 [8, 2048, 4096], P(None, 'gy', 'gx'), may hold values from 0.5 to 2
- soil_wetness: float32 [8, 16, 256, 512], P('gx', 'gy'), may hold values from 0.1 to 1
- surface_table: float32 [5, 4], replicated, may hold values from 0.3 to 1.5
Outputs:
- skin: float32 [2048, 4096], P('gy', 'gx')
- substrate_out: float32 [8, 2048, 4096], P(None, 'gy', 'gx')
Inputs may be any that keep to these rules, and one draw needn't show every extreme that they name: The rows of one device name any one owner at most 2 times; some owner is named exactly 2 times.
All inputs are finite; a program needn't handle non-finite values.
Results may differ from a plain program's by a relative error of at most 0.0003.
Values sent between devices are 32-bit elements; how exact they have to be, the bound alone decides.
A program may use at most 128 MiB of HBM per device.

v0:
```python
import jax
import jax.numpy as jnp
from jax import lax
from jax.sharding import PartitionSpec as P

NEWTON = 6


def padded_2(block, sides, width):
    for axis, dim in sides:
        count = lax.axis_size(axis)
        forward = [(i, i + 1) for i in range(count - 1)]
        forward.append((count - 1, 0))
        backward = [(target, source) for source, target in forward]
        low = lax.ppermute(
            lax.slice_in_dim(block, block.shape[dim] - width, None, axis=dim), axis, forward
        )
        high = lax.ppermute(lax.slice_in_dim(block, 0, width, axis=dim), axis, backward)
        block = jnp.concatenate([low, block, high], axis=dim)
    return block


def regrid(coarse, index_list, tables):
    tile_rows = coarse.shape[0]
    fine_flux = jnp.zeros((tile_rows, 3, tables.shape[2]), jnp.float32)
    for tile_pick in range(tables.shape[0]):
        weight_uses = jnp.sum((index_list == tile_pick).astype(jnp.float32), axis=1)
        weighted = coarse * weight_uses[:, None, None]
        fine_flux = fine_flux + jnp.einsum(
            "rcp,ps->rcs", weighted, tables[tile_pick], precision=lax.Precision.HIGHEST
        )
    return fine_flux


def balance(forcing, top_layer, surface_kinds, wetness, surface_table):

    def lookup(field_row):
        table_sum = jnp.zeros(top_layer.shape, jnp.float32)
        for surface_kind in range(surface_table.shape[1]):
            table_sum = table_sum + jnp.where(
                surface_kinds == surface_kind, surface_table[field_row, surface_kind], 0.0
            )
        return table_sum

    absorb, emit, sensible, beta, conduct = [lookup(field_row) for field_row in range(5)]
    air_temp = 1.0 + 0.2 * forcing[:, 0]
    vapour = 0.2 * forcing[:, 1]
    radiation = 2.0 + 0.3 * forcing[:, 2]
    skin_temp = top_layer
    for iteration in range(NEWTON):
        moisture = beta * wetness * jnp.exp(1.5 * (skin_temp - 1.0))
        magnitude = jnp.abs(skin_temp)
        theta_cube = magnitude * magnitude * magnitude
        residual_f = (
            absorb * radiation
            - emit * skin_temp * theta_cube
            - sensible * (skin_temp - air_temp)
            - (moisture - beta * wetness * vapour)
            - conduct * (skin_temp - top_layer)
        )
        slope_sum = 4.0 * emit * theta_cube + sensible + 1.5 * moisture + conduct
        skin_temp = skin_temp + 0.4 * residual_f / slope_sum
    ground = conduct * (skin_temp - top_layer)
    return (skin_temp, ground)


def per_device(
    panels,
    regrid_tiles,
    weight_index,
    owner,
    surface_type,
    substrate,
    conductivity,
    soil_wetness,
    surface_table,
):
    tile_rows = substrate.shape[1]
    devices = lax.axis_size("gx") * lax.axis_size("gy")
    slot_total = soil_wetness.shape[2]
    capacity = slot_total // devices
    padded = padded_2(substrate, (("gy", 1), ("gx", 2)), 1)
    lateral = (
        padded[:, 2:, 1:-1]
        + padded[:, :-2, 1:-1]
        + padded[:, 1:-1, 2:]
        + padded[:, 1:-1, :-2]
        - 4.0 * substrate
    )
    layer_above = jnp.concatenate([substrate[:1], substrate[:-1]], axis=0)
    layer_below = jnp.concatenate([substrate[1:], substrate[-1:]], axis=0)
    vertical = layer_above + layer_below - 2.0 * substrate
    diffused = substrate + 0.08 * conductivity * (lateral + vertical)
    destination = owner[0, :, 0]
    same_owner = destination[:, None] == destination[None, :]
    earlier = lax.broadcasted_iota(jnp.int32, (tile_rows, tile_rows), 0) > lax.broadcasted_iota(
        jnp.int32, (tile_rows, tile_rows), 1
    )
    tile_rank = jnp.sum((same_owner & earlier).astype(jnp.int32), axis=1)
    slot_of = destination * capacity + tile_rank

    def to_slots(values):
        blank_buf = jnp.zeros((slot_total,) + values.shape[1:], values.dtype)
        return blank_buf.at[slot_of].set(values)

    coarse = jnp.repeat(panels, 2, axis=1).transpose(1, 0, 2)
    top_layer = diffused[0]
    index_list = weight_index[0]
    fine_flux = regrid(coarse, index_list, regrid_tiles)
    got_flux, got_top, got_kinds = (
        lax.all_to_all(to_slots(fine_flux), ("gx", "gy"), split_axis=0, concat_axis=0, tiled=True),
        lax.all_to_all(to_slots(top_layer), ("gx", "gy"), split_axis=0, concat_axis=0, tiled=True),
        lax.all_to_all(
            to_slots(surface_type), ("gx", "gy"), split_axis=0, concat_axis=0, tiled=True
        ),
    )
    skin_slots, ground_slots = balance(
        got_flux, got_top, got_kinds, soil_wetness[0, 0], surface_table
    )
    back_skin, back_ground = (
        lax.all_to_all(skin_slots, ("gx", "gy"), split_axis=0, concat_axis=0, tiled=True),
        lax.all_to_all(ground_slots, ("gx", "gy"), split_axis=0, concat_axis=0, tiled=True),
    )
    skin_out = back_skin[slot_of]
    ground_rows = back_ground[slot_of]
    substrate_out = diffused.at[0].add(0.5 * ground_rows)
    return (skin_out, substrate_out)


def solution(mesh):
    placed = (
        P(None, "gy", "gx"),
        P(),
        P("gx", "gy", None),
        P("gx", "gy", None),
        P("gy", "gx"),
        P(None, "gy", "gx"),
        P(None, "gy", "gx"),
        P("gx", "gy", None, None),
        P(),
    )
    return jax.shard_map(
        per_device,
        mesh=mesh,
        in_specs=placed,
        out_specs=(P("gy", "gx"), P(None, "gy", "gx")),
        check_vma=False,
    )
```

profile of v0, /device:TPU:1, one launch (start us, length us, event | category | flops | bytes accessed | tf_op | source)
XLA Modules:
  0.0 184.8 jit_solution(7672569054861644587)
XLA Ops:
  0.6 0.9 convert_reduce_fusion
  1.6 0.7 fusion.138
  2.2 1.6 scatter_custom_fusion.1
  3.8 1.1 all_to_all.29
  4.9 11.5 %all-to-all-start.1 = ((s32[128,2,512]{2,1,0:T(2,128)}), s32[128,2,512]{2,1,0:T(2,128)S(1)}, u32[]{:S(2)}, u32[]{:S(2)}) async-start(s32[128,2,512]{2,1,0:T(2,128)} %all_to_all.29), calls=%async_computation.1 | async-start | bytes 1048576 | tf_op jit(solution)/shard_map/all_to_all | solution.py:113
  16.4 0.1 broadcast_in_dim.121
  16.5 0.3 reshape.165
  16.9 2.0 %fusion.28 = f32[128,3,512]{2,0,1:T(8,128)S(1)} fusion(f32[16,256,512]{2,1,0:T(8,128)} %param.12, f32[3,128,256]{2,1,0:T(8,128)S(1)} %reshape.165, f32[128]{0:T(128)S(1)} %get-tuple-element.31), kind=kOutput, calls=%fused_computation.63 | convolution fusion | flops 604078080 | bytes 1704448 | tf_op jit(solution)/shard_map/rcp,ps->rcs/dot_general | solution.py:29
  18.9 2.4 %convolution_add_fusion.14 = f32[128,3,512]{2,0,1:T(8,128)S(1)} fusion(f32[128,3,512]{2,0,1:T(8,128)S(1)} %fusion.28, f32[16,256,512]{2,1,0:T(8,128)} %param.12, f32[3,128,256]{2,1,0:T(8,128)S(1)} %reshape.165, f32[128]{0:T(128)S(1)} %get-tuple-element.30), kind=kOutput, calls=%fused_computation.36 | convolution fusion | flops 604274688 | bytes 2490880 | tf_op jit(solution)/shard_map/rcp,ps->rcs/dot_general | solution.py:29
  21.3 1.9 %convolution_add_fusion.13 = f32[128,3,512]{2,0,1:T(8,128)S(1)} fusion(f32[128,3,512]{2,0,1:T(8,128)S(1)} %convolution_add_fusion.14, f32[16,256,512]{2,1,0:T(8,128)} %param.12, f32[3,128,256]{2,1,0:T(8,128)S(1)} %reshape.165, f32[128]{0:T(128)S(1)} %get-tuple-element.29), kind=kOutput, calls=%fused_computation.35 | convolution fusion | flops 604274688 | bytes 2490880 | tf_op jit(solution)/shard_map/rcp,ps->rcs/dot_general | solution.py:29
  23.2 1.9 %convolution_add_fusion.12 = f32[128,3,512]{2,0,1:T(8,128)S(1)} fusion(f32[128,3,512]{2,0,1:T(8,128)S(1)} %convolution_add_fusion.13, f32[16,256,512]{2,1,0:T(8,128)} %param.12, f32[3,128,256]{2,1,0:T(8,128)S(1)} %reshape.165, f32[128]{0:T(128)S(1)} %get-tuple-element.28), kind=kOutput, calls=%fused_computation.34 | convolution fusion | flops 604274688 | bytes 2490880 | tf_op jit(solution)/shard_map/rcp,ps->rcs/dot_general | solution.py:29
  25.1 0.8 convolution_add_fusion.11
  25.9 0.8 convolution_add_fusion.10
  26.8 0.8 convolution_add_fusion.9
  27.6 0.8 convolution_add_fusion.8
  28.5 0.8 convolution_add_fusion.7
  29.3 0.8 convolution_add_fusion.6
  30.1 0.8 convolution_add_fusion.5
  31.0 0.8 convolution_add_fusion.4
  31.8 0.8 convolution_add_fusion.3
  32.7 0.8 convolution_add_fusion.2
  33.5 1.0 convolution_add_fusion.1
  34.5 0.8 convolution_add_fusion
  35.4 0.5 copy.53
  35.9 1.6 broadcast_in_dim.120
  37.5 13.7 %scatter_fusion = f32[256,3,512]{2,1,0:T(4,128)} fusion(f32[256,3,512]{2,1,0:T(4,128)} %broadcast_in_dim.120, s32[128]{0:T(128)S(1)} %fusion.138, f32[128,3,512]{2,1,0:T(4,128)S(1)} %copy.53), kind=kCustom, calls=%fused_computation.4 | custom fusion | bytes 2359808 | tf_op jit(solution)/shard_map/scatter | solution.py:104
  51.2 0.8 copy-done.2
  52.0 10.2 %all-to-all-start.2 = ((f32[256,3,512]{2,1,0:T(4,128)}), f32[256,3,512]{2,1,0:T(4,128)}, u32[]{:S(2)}, u32[]{:S(2)}) async-start(f32[256,3,512]{2,1,0:T(4,128)} %scatter_fusion), calls=%async_computation.2 | async-start | bytes 4194304 | tf_op jit(solution)/shard_map/all_to_all | solution.py:111
  62.3 4.9 %collective-permute-start = (f32[8,1,512]{2,1,0:T(1,128)S(1)}, f32[8,1,512]{2,1,0:T(1,128)S(1)}, u32[]{:S(2)}, u32[]{:S(2)}) collective-permute-start(f32[8,1,512]{2,1,0:T(1,128)S(1)} %get-tuple-element.42), channel_id=1, source_target_pairs={{1,0},{2,1},{3,2},{4,3},{5,4},{6,5},{7,6},{8,7},{9,8},{10,9},{11,1... | collective-permute-start | bytes 49160 | tf_op jit(solution)/shard_map/ppermute | solution.py:18
  67.2 2.4 %fusion.139 = (f32[7,128,512]{2,1,0:T(8,128)}, f32[7,128,512]{2,1,0:T(8,128)}) fusion(f32[8,128,512]{2,1,0:T(8,128)S(1)} %copy-done), kind=kLoop, calls=%fused_computation.210 | loop fusion | bytes 7340032 | tf_op jit(solution)/shard_map/slice | solution.py:91
  69.6 0.7 fusion.140
  70.3 15.9 %collective-permute-done = f32[8,1,512]{2,1,0:T(1,128)S(1)} collective-permute-done((f32[8,1,512]{2,1,0:T(1,128)S(1)}, f32[8,1,512]{2,1,0:T(1,128)S(1)}, u32[]{:S(2)}, u32[]{:S(2)}) %collective-permute-start) | collective-permute-done | bytes 16416 | tf_op jit(solution)/shard_map/ppermute | solution.py:18
  86.2 2.5 %collective-permute-done.1 = f32[8,1,512]{2,1,0:T(1,128)S(1)} collective-permute-done((f32[8,1,512]{2,1,0:T(1,128)S(1)}, f32[8,1,512]{2,1,0:T(1,128)S(1)}, u32[]{:S(2)}, u32[]{:S(2)}) %collective-permute-start.1) | collective-permute-done | bytes 16416 | tf_op jit(solution)/shard_map/ppermute | solution.py:15
  88.7 0.2 pad_maximum_fusion.10
  89.0 0.3 copy.47
  89.3 2.6 %collective-permute-start.3 = (f32[8,130,1]{1,0,2:T(8,128)S(1)}, f32[8,130,1]{1,0,2:T(8,128)S(1)}, u32[]{:S(2)}, u32[]{:S(2)}) collective-permute-start(f32[8,130,1]{1,0,2:T(8,128)S(1)} %copy.47), channel_id=1, source_target_pairs={{0,16},{16,32},{32,48},{48,64},{64,80},{80,96},{96,112},{112,0},{1... | collective-permute-start | bytes 12488 | tf_op jit(solution)/shard_map/ppermute | solution.py:15
  92.0 0.3 copy.45
  92.3 0.7 fusion.142
  93.0 0.6 slice.230
  93.6 2.2 %squeeze.152 = f32[128,2,512]{2,1,0:T(2,128)} reshape(f32[1,1,256,512]{3,2,1,0:T(8,128)} %param.18) | data formatting | bytes 1048576 | tf_op jit(solution)/shard_map/squeeze | solution.py:118
  95.8 0.2 copy.48
  96.1 0.2 copy.46
  96.3 6.4 %fusion.4 = f32[8,128,512]{2,1,0:T(8,128)} fusion(f32[8,128,512]{2,1,0:T(8,128)S(1)} %copy-done, f32[8,130,1]{2,1,0:T(8,128)S(1)} %copy.48, f32[8,1,512]{2,1,0:T(1,128)S(1)} %collective-permute-done, f32[8,1,512]{2,1,0:T(1,128)S(1)} %collective-permute-done.1, f32[8,130,1]{2,1,0:T(8,128)S(1)} %copy.46, f32[7,128,512]{2,1,0:T(8,128)} %get-tuple-element.38, ...), kind=kLoop, calls=%fused_computation.10 | loop fusion | flops 11534336 | bytes 10526848 | tf_op jit(solution)/shard_map/add | solution.py:93
  102.7 1.6 scatter_custom_fusion
  104.4 1.1 all_to_all.27
  105.5 6.3 %all-to-all-start = ((f32[128,2,512]{2,1,0:T(2,128)}), f32[128,2,512]{2,1,0:T(2,128)S(1)}, u32[]{:S(2)}, u32[]{:S(2)}) async-start(f32[128,2,512]{2,1,0:T(2,128)} %all_to_all.27), calls=%async_computation | async-start | bytes 1048576 | tf_op jit(solution)/shard_map/all_to_all | solution.py:112
  111.8 0.9 copy_compare_fusion.3
  112.7 8.1 %fusion.12 = (f32[256,512]{1,0:T(8,128)S(1)}, f32[256,512]{1,0:T(8,128)S(1)}, f32[256,512]{1,0:T(8,128)S(1)}) fusion(f32[256,3,512]{2,1,0:T(4,128)} %all-to-all-done.2), kind=kLoop, calls=%fused_computation.47 | loop fusion | flops 655360 | bytes 3145728 | tf_op jit(solution)/shard_map/add | solution.py:48
  120.9 0.3 mul.701
  121.2 0.3 add.362
  121.5 0.3 add.354
  121.8 3.9 %all-to-all-done = f32[128,2,512]{2,1,0:T(2,128)S(1)} async-done(((f32[128,2,512]{2,1,0:T(2,128)}), f32[128,2,512]{2,1,0:T(2,128)S(1)}, u32[]{:S(2)}, u32[]{:S(2)}) %all-to-all-start) | async-done | bytes 524320 | tf_op jit(solution)/shard_map/all_to_all | solution.py:112
  125.7 17.0 %subtract_multiply_fusion = (f32[128,2,512]{2,0,1:T(8,128)S(1)}, f32[128,2,512]{2,0,1:T(8,128)S(1)}) fusion(f32[128,2,512]{2,1,0:T(2,128)S(1)} %all-to-all-done, pred[128,2,512]{2,0,1:T(8,128)(4,1)} %get-tuple-element.46, pred[128,2,512]{2,0,1:T(8,128)(4,1)S(1)} %get-tuple-element.45, pred[128,2,512]{2,0,1:T(8,128)(4,1)S(1)} %get-tuple-element.44, ...), kind=kLoop, calls=%fused_computation.68 | loop fusion | flops 25034752 | bytes 4194384 | tf_op jit(solution)/shard_map/mul | solution.py:63
  142.7 1.2 copy.77
  143.9 6.0 %all-to-all-start.3 = ((f32[128,2,512]{2,1,0:T(2,128)}), f32[128,2,512]{2,1,0:T(2,128)S(1)}, u32[]{:S(2)}, u32[]{:S(2)}) async-start(f32[128,2,512]{2,1,0:T(2,128)} %copy.77), calls=%async_computation.3 | async-start | bytes 1048576 | tf_op jit(solution)/shard_map/all_to_all | solution.py:121
  149.9 1.2 copy.79
  151.1 12.7 %all-to-all-done.3 = f32[128,2,512]{2,1,0:T(2,128)S(1)} async-done(((f32[128,2,512]{2,1,0:T(2,128)}), f32[128,2,512]{2,1,0:T(2,128)S(1)}, u32[]{:S(2)}, u32[]{:S(2)}) %all-to-all-start.3) | async-done | bytes 524320 | tf_op jit(solution)/shard_map/all_to_all | solution.py:121
  163.8 4.2 %all-to-all-start.4 = ((f32[128,2,512]{2,1,0:T(2,128)}), f32[128,2,512]{2,1,0:T(2,128)S(1)}, u32[]{:S(2)}, u32[]{:S(2)}) async-start(f32[128,2,512]{2,1,0:T(2,128)} %copy.79), calls=%async_computation.4 | async-start | bytes 1048576 | tf_op jit(solution)/shard_map/all_to_all | solution.py:122
  168.0 0.4 all_to_all.33
  168.3 1.5 gather_fusion
  169.8 12.2 %all-to-all-done.4 = f32[128,2,512]{2,1,0:T(2,128)S(1)} async-done(((f32[128,2,512]{2,1,0:T(2,128)}), f32[128,2,512]{2,1,0:T(2,128)S(1)}, u32[]{:S(2)}, u32[]{:S(2)}) %all-to-all-start.4) | async-done | bytes 524320 | tf_op jit(solution)/shard_map/all_to_all | solution.py:122
  182.0 0.4 all_to_all.35
  182.4 0.8 gather_fusion.1
  183.1 1.7 fusion.98
  (24 shorter events, 0.1 us)
Async XLA Ops:
  0.6 15.8 %copy-start.5 = (f32[3,64,256]{2,1,0:T(8,128)S(1)}, f32[3,64,256]{2,1,0:T(8,128)}, u32[]{:S(2)}) copy-start(f32[3,64,256]{2,1,0:T(8,128)} %param.11) | copy-start | bytes 589828
  0.6 16.2 %copy-start.7 = (s32[1,128,2]{1,2,0:T(2,128)S(1)}, s32[1,128,2]{1,2,0:T(2,128)}, u32[]{:S(2)}) copy-start(s32[1,128,2]{1,2,0:T(2,128)} %param.13) | copy-start | bytes 3076
  4.9 46.3 %all-to-all-start.1 = ((s32[128,2,512]{2,1,0:T(2,128)}), s32[128,2,512]{2,1,0:T(2,128)S(1)}, u32[]{:S(2)}, u32[]{:S(2)}) async-start(s32[128,2,512]{2,1,0:T(2,128)} %all_to_all.29), calls=%async_computation.1 | async-start | bytes 1048576 | tf_op jit(solution)/shard_map/all_to_all | solution.py:113
  16.9 8.2 %copy-start.1 = (f32[16,256,512]{2,1,0:T(8,128)S(1)}, f32[16,256,512]{2,1,0:T(8,128)}, u32[]{:S(2)}) copy-start(f32[16,256,512]{2,1,0:T(8,128)} %param.12) | copy-start | bytes 25165828
  51.2 11.0 %copy-start = (f32[8,128,512]{2,1,0:T(8,128)S(1)}, f32[8,128,512]{2,1,0:T(8,128)}, u32[]{:S(2)}) copy-start(f32[8,128,512]{2,1,0:T(8,128)} %param.16) | copy-start | bytes 6291460
  51.2 0.8 copy-start.2
  52.0 53.4 %all-to-all-start.2 = ((f32[256,3,512]{2,1,0:T(4,128)}), f32[256,3,512]{2,1,0:T(4,128)}, u32[]{:S(2)}, u32[]{:S(2)}) async-start(f32[256,3,512]{2,1,0:T(4,128)} %scatter_fusion), calls=%async_computation.2 | async-start | bytes 4194304 | tf_op jit(solution)/shard_map/all_to_all | solution.py:111
  62.3 23.9 %collective-permute-start = (f32[8,1,512]{2,1,0:T(1,128)S(1)}, f32[8,1,512]{2,1,0:T(1,128)S(1)}, u32[]{:S(2)}, u32[]{:S(2)}) collective-permute-start(f32[8,1,512]{2,1,0:T(1,128)S(1)} %get-tuple-element.42), channel_id=1, source_target_pairs={{1,0},{2,1},{3,2},{4,3},{5,4},{6,5},{7,6},{8,7},{9,8},{10,9},{11,1... | collective-permute-start | bytes 49160 | tf_op jit(solution)/shard_map/ppermute | solution.py:18
  67.2 21.6 %collective-permute-start.1 = (f32[8,1,512]{2,1,0:T(1,128)S(1)}, f32[8,1,512]{2,1,0:T(1,128)S(1)}, u32[]{:S(2)}, u32[]{:S(2)}) collective-permute-start(f32[8,1,512]{2,1,0:T(1,128)S(1)} %get-tuple-element.41), channel_id=1, source_target_pairs={{0,1},{1,2},{2,3},{3,4},{4,5},{5,6},{6,7},{7,8},{8,9},{9,10},{10,1... | collective-permute-start | bytes 49160 | tf_op jit(solution)/shard_map/ppermute | solution.py:15
  70.3 22.0 %copy-start.6 = (f32[5,4]{0,1:T(4,128)S(1)}, f32[5,4]{0,1:T(4,128)}, u32[]{:S(2)}) copy-start(f32[5,4]{0,1:T(4,128)} %param.19) | copy-start | bytes 244
  89.3 6.5 %collective-permute-start.3 = (f32[8,130,1]{1,0,2:T(8,128)S(1)}, f32[8,130,1]{1,0,2:T(8,128)S(1)}, u32[]{:S(2)}, u32[]{:S(2)}) collective-permute-start(f32[8,130,1]{1,0,2:T(8,128)S(1)} %copy.47), channel_id=1, source_target_pairs={{0,16},{16,32},{32,48},{48,64},{64,80},{80,96},{96,112},{112,0},{1... | collective-permute-start | bytes 12488 | tf_op jit(solution)/shard_map/ppermute | solution.py:15
  92.3 3.8 %collective-permute-start.2 = (f32[8,130,1]{1,0,2:T(8,128)S(1)}, f32[8,130,1]{1,0,2:T(8,128)S(1)}, u32[]{:S(2)}, u32[]{:S(2)}) collective-permute-start(f32[8,130,1]{1,0,2:T(8,128)S(1)} %copy.45), channel_id=1, source_target_pairs={{16,0},{32,16},{48,32},{64,48},{80,64},{96,80},{112,96},{0,112},{1... | collective-permute-start | bytes 12488 | tf_op jit(solution)/shard_map/ppermute | solution.py:18
  102.7 9.0 %copy-start.3 = (s32[128,2,512]{2,1,0:T(2,128)S(1)}, s32[128,2,512]{2,1,0:T(2,128)}, u32[]{:S(2)}) copy-start(s32[128,2,512]{2,1,0:T(2,128)} %copy-done.2) | copy-start | bytes 1572868
  105.5 20.2 %all-to-all-start = ((f32[128,2,512]{2,1,0:T(2,128)}), f32[128,2,512]{2,1,0:T(2,128)S(1)}, u32[]{:S(2)}, u32[]{:S(2)}) async-start(f32[128,2,512]{2,1,0:T(2,128)} %all_to_all.27), calls=%async_computation | async-start | bytes 1048576 | tf_op jit(solution)/shard_map/all_to_all | solution.py:112
  120.9 4.8 %copy-start.4 = (f32[128,2,512]{2,1,0:T(2,128)S(1)}, f32[128,2,512]{2,1,0:T(2,128)}, u32[]{:S(2)}) copy-start(f32[128,2,512]{2,1,0:T(2,128)} %squeeze.152) | copy-start | bytes 1572868
  143.9 19.9 %all-to-all-start.3 = ((f32[128,2,512]{2,1,0:T(2,128)}), f32[128,2,512]{2,1,0:T(2,128)S(1)}, u32[]{:S(2)}, u32[]{:S(2)}) async-start(f32[128,2,512]{2,1,0:T(2,128)} %copy.77), calls=%async_computation.3 | async-start | bytes 1048576 | tf_op jit(solution)/shard_map/all_to_all | solution.py:121
  163.8 18.2 %all-to-all-start.4 = ((f32[128,2,512]{2,1,0:T(2,128)}), f32[128,2,512]{2,1,0:T(2,128)S(1)}, u32[]{:S(2)}, u32[]{:S(2)}) async-start(f32[128,2,512]{2,1,0:T(2,128)} %copy.79), calls=%async_computation.4 | async-start | bytes 1048576 | tf_op jit(solution)/shard_map/all_to_all | solution.py:122
where the time goes:
time: 186 us; the launch traced here: 185 us
  waiting for transfers between devices  47.2 us (25%)
  starting transfers between devices  45.6 us (25%)
  local copies, waits for them, and re-layouts  36.5 us (20%)
  other arithmetic  36 us (19%)
  matrix products  18.4 us (10%)
    dot_general x16, matrix products, regrid(): jnp.einsum('rcp,ps->rcs', weighted, tables[tile_pick], precision=lax.Prec...  18.4 us
    mul x1, other arithmetic, balance(): ground = conduct * (skin_temp - top_layer)  17 us
    scatter x3, local copies, waits for them, and re-layouts, to_slots(): return blank_buf.at[slot_of].set(values)  16.9 us
    ppermute x2, waiting for transfers between devices, padded_2(): lax.ppermute(lax.slice_in_dim(block, 0, width, axis=dim), axis, backward)  15.9 us
    all_to_all x1, waiting for transfers between devices, per_device(): lax.all_to_all(skin_slots, ('gx', 'gy'), split_axis=0, concat_axis=0, til...  12.7 us
    all_to_all x1, waiting for transfers between devices, per_device(): lax.all_to_all(ground_slots, ('gx', 'gy'), split_axis=0, concat_axis=0, t...  12.2 us
    all_to_all x1, starting transfers between devices, per_device(): lax.all_to_all(to_slots(surface_type), ('gx', 'gy'), split_axis=0, concat...  11.5 us
    all_to_all x1, starting transfers between devices, per_device(): lax.all_to_all(to_slots(fine_flux), ('gx', 'gy'), split_axis=0, concat_ax...  10.2 us
  transfers between devices with their start and end apart: 9, of which 5 were waited for; matrix products, arithmetic and copies ran while one was open for 34% of the time, Pallas kernels for 0%

commit v1 on v0

v1 whole, which is shorter than its diff:
```python
import jax
import jax.numpy as jnp
from jax import lax
from jax.sharding import PartitionSpec as P

NEWTON = 6


def halo(edge, axis, step):
    count = lax.axis_size(axis)
    return lax.ppermute(edge, axis, [(i, (i + step) % count) for i in range(count)])


def regrid(panels, index_list, tables):
    fields, coarse_rows, half = panels.shape
    tiles, _, width = tables.shape
    flat = panels.reshape(fields * coarse_rows, half)
    total = jnp.zeros((fields, coarse_rows, 2, width), jnp.float32)
    for pick in range(tiles):
        uses = jnp.sum((index_list == pick).astype(jnp.float32), axis=1).reshape(1, coarse_rows, 2, 1)
        product = jnp.dot(flat, tables[pick], precision=lax.Precision.HIGHEST)
        total = total + uses * product.reshape(fields, coarse_rows, 1, width)
    return total.reshape(fields, coarse_rows * 2, width)


def balance(forcing, top_layer, surface_kinds, wetness, surface_table):
    def lookup(field_row):
        table_sum = jnp.zeros(top_layer.shape, jnp.float32)
        for surface_kind in range(surface_table.shape[1]):
            table_sum = table_sum + jnp.where(
                surface_kinds == surface_kind, surface_table[field_row, surface_kind], 0.0
            )
        return table_sum

    absorb, emit, sensible, beta, conduct = [lookup(field_row) for field_row in range(5)]
    air_temp = 1.0 + 0.2 * forcing[0]
    vapour = 0.2 * forcing[1]
    radiation = 2.0 + 0.3 * forcing[2]
    skin_temp = top_layer
    for iteration in range(NEWTON):
        moisture = beta * wetness * jnp.exp(1.5 * (skin_temp - 1.0))
        magnitude = jnp.abs(skin_temp)
        theta_cube = magnitude * magnitude * magnitude
        residual_f = (
            absorb * radiation
            - emit * skin_temp * theta_cube
            - sensible * (skin_temp - air_temp)
            - (moisture - beta * wetness * vapour)
            - conduct * (skin_temp - top_layer)
        )
        slope_sum = 4.0 * emit * theta_cube + sensible + 1.5 * moisture + conduct
        skin_temp = skin_temp + 0.4 * residual_f / slope_sum
    return skin_temp, conduct * (skin_temp - top_layer)


def per_device(
    panels,
    regrid_tiles,
    weight_index,
    owner,
    surface_type,
    substrate,
    conductivity,
    soil_wetness,
    surface_table,
):
    tile_rows = substrate.shape[1]
    handed = lax.all_to_all(soil_wetness[0, 0], ("gx", "gy"), split_axis=0, concat_axis=0, tiled=True)
    north = halo(substrate[:, -1:, :], "gy", 1)
    south = halo(substrate[:, :1, :], "gy", -1)
    west = halo(substrate[:, :, -1:], "gx", 1)
    east = halo(substrate[:, :, :1], "gx", -1)
    lateral = (
        jnp.concatenate([substrate[:, 1:], south], axis=1)
        + jnp.concatenate([north, substrate[:, :-1]], axis=1)
        + jnp.concatenate([substrate[:, :, 1:], east], axis=2)
        + jnp.concatenate([west, substrate[:, :, :-1]], axis=2)
        - 4.0 * substrate
    )
    layer_above = jnp.concatenate([substrate[:1], substrate[:-1]], axis=0)
    layer_below = jnp.concatenate([substrate[1:], substrate[-1:]], axis=0)
    vertical = layer_above + layer_below - 2.0 * substrate
    diffused = substrate + 0.08 * conductivity * (lateral + vertical)
    destination = owner[0, :, 0]
    same_owner = destination[:, None] == destination[None, :]
    earlier = lax.broadcasted_iota(jnp.int32, (tile_rows, tile_rows), 0) > lax.broadcasted_iota(
        jnp.int32, (tile_rows, tile_rows), 1
    )
    tile_rank = jnp.sum((same_owner & earlier).astype(jnp.int32), axis=1)
    wetness = handed[destination * 2 + tile_rank]
    fine_flux = regrid(panels, weight_index[0], regrid_tiles)
    skin, ground = balance(fine_flux, diffused[0], surface_type, wetness, surface_table)
    return skin, diffused.at[0].add(0.5 * ground)


def solution(mesh):
    placed = (
        P(None, "gy", "gx"),
        P(),
        P("gx", "gy", None),
        P("gx", "gy", None),
        P("gy", "gx"),
        P(None, "gy", "gx"),
        P(None, "gy", "gx"),
        P("gx", "gy", None, None),
        P(),
    )
    return jax.shard_map(
        per_device,
        mesh=mesh,
        in_specs=placed,
        out_specs=(P("gy", "gx"), P(None, "gy", "gx")),
        check_vma=False,
    )
```

time: 186 us -> 127 us (0.68)
  waiting for transfers between devices: 47.2 us -> 0.01 us
  starting transfers between devices: 45.6 us -> 18.2 us
  matrix products: 18.4 us -> 28.6 us
  local copies, waits for them, and re-layouts: 36.5 us -> 44.3 us
  other arithmetic: 36 us -> 33.5 us
    all_to_all x5 -> x1, waiting for transfers between devices: 28.8 us -> 0.01 us  [per_device(): lax.all_to_all(soil_wetness[0, 0], ('gx', 'gy'), split_axis=0, concat_axi...]
    all_to_all x5 -> x1, starting transfers between devices: 38.1 us -> 10.3 us  [per_device(): lax.all_to_all(soil_wetness[0, 0], ('gx', 'gy'), split_axis=0, concat_axi...]
    mul x2 -> x17, local copies, waits for them, and re-layouts: 1.52 us -> 21.9 us  [the longest x16 20 us: regrid(): total = total + uses * product.reshape(fields, coarse_rows, 1, width)]
    ppermute x4, waiting for transfers between devices: 18.4 us -> 0.01 us  [halo(): lax.ppermute(edge, axis, [(i, (i + step) % count) for i in range(count)])]
    mul x1 -> x0, other arithmetic: 17 us -> none  [balance(): ground = conduct * (skin_temp - top_layer)]
    scatter x3 -> x0, local copies, waits for them, and re-layouts: 16.9 us -> none  [to_slots(): return blank_buf.at[slot_of].set(values)]
    add x1 -> x3, other arithmetic: 8.14 us -> 23.1 us  [the longest x1 15.6 us: balance(): skin_temp = skin_temp + 0.4 * residual_f / slope_sum]
    dot_general x16, matrix products: 18.4 us -> 28.6 us  [regrid(): product = jnp.dot(flat, tables[pick], precision=lax.Precision.HIGHEST)]
  transfers between devices with their start and end apart: 9 -> 5, of which waited for: 5 -> 0; matrix products, arithmetic and copies ran while one was open for 34% -> 63% of each run, Pallas kernels for 0% -> 0%
where the time goes in v1:
time: 127 us; the launch traced here: 126 us
  local copies, waits for them, and re-layouts  44.3 us (35%)
  other arithmetic  33.5 us (26%)
  matrix products  28.6 us (23%)
  starting transfers between devices  18.2 us (14%)
    dot_general x16, matrix products, regrid(): product = jnp.dot(flat, tables[pick], precision=lax.Precision.HIGHEST)  28.6 us
    mul x16, local copies, waits for them, and re-layouts, regrid(): total = total + uses * product.reshape(fields, coarse_rows, 1, width)  20 us
    add x1, other arithmetic, balance(): skin_temp = skin_temp + 0.4 * residual_f / slope_sum  15.6 us
    all_to_all x1, starting transfers between devices, per_device(): lax.all_to_all(soil_wetness[0, 0], ('gx', 'gy'), split_axis=0, concat_axi...  10.3 us
    ppermute x4, starting transfers between devices, halo(): lax.ppermute(edge, axis, [(i, (i + step) % count) for i in range(count)])  7.96 us
    add x1, other arithmetic, per_device(): diffused = substrate + 0.08 * conductivity * (lateral + vertical)  6.82 us
    add x1, other arithmetic, regrid(): total = total + uses * product.reshape(fields, coarse_rows, 1, width)  6.23 us
    slice x2, local copies, waits for them, and re-layouts, per_device(): layer_below = jnp.concatenate([substrate[1:], substrate[-1:]], axis=0)  3.09 us
  transfers between devices with their start and end apart: 5, of which 0 were waited for; matrix products, arithmetic and copies ran while one was open for 63% of the time, Pallas kernels for 0%

profile of v1, /device:TPU:1, one launch (start us, length us, event | category | flops | bytes accessed | tf_op | source)
XLA Modules:
  0.0 125.6 jit_solution(18210519259736703495)
XLA Ops:
  0.6 0.0 copy-start
  0.7 2.5 %fusion.131 = (f32[8,128,1]{2,1,0:T(8,128)}, f32[8,128,1]{2,1,0:T(8,128)}) fusion(f32[8,128,512]{2,1,0:T(8,128)} %param.16), kind=kLoop, calls=%fused_computation.181 | loop fusion | bytes 16384 | tf_op jit(solution)/shard_map/slice | solution.py:71
  3.1 1.4 %collective-permute-start.2 = (f32[8,128,1]{2,1,0:T(8,128)}, f32[8,128,1]{2,1,0:T(8,128)}, u32[]{:S(2)}, u32[]{:S(2)}) collective-permute-start(f32[8,128,1]{2,1,0:T(8,128)} %get-tuple-element.40), channel_id=1, source_target_pairs={{0,112},{16,0},{32,16},{48,32},{64,48},{80,64},{96,80},{112,96},{1... | collective-permute-start | bytes 12296 | tf_op jit(solution)/shard_map/ppermute | solution.py:11
  4.5 1.6 %collective-permute-start.3 = (f32[8,128,1]{2,1,0:T(8,128)}, f32[8,128,1]{2,1,0:T(8,128)}, u32[]{:S(2)}, u32[]{:S(2)}) collective-permute-start(f32[8,128,1]{2,1,0:T(8,128)} %get-tuple-element.39), channel_id=1, source_target_pairs={{0,16},{16,32},{32,48},{48,64},{64,80},{80,96},{96,112},{112,0},{1... | collective-permute-start | bytes 12296 | tf_op jit(solution)/shard_map/ppermute | solution.py:11
  6.2 0.6 fusion.133
  6.8 4.9 %collective-permute-start = (f32[8,1,512]{2,1,0:T(1,128)}, f32[8,1,512]{2,1,0:T(1,128)S(1)}, u32[]{:S(2)}, u32[]{:S(2)}) collective-permute-start(f32[8,1,512]{2,1,0:T(1,128)} %get-tuple-element.44), channel_id=1, source_target_pairs={{0,15},{1,0},{2,1},{3,2},{4,3},{5,4},{6,5},{7,6},{8,7},{9,8},{10,9... | collective-permute-start | bytes 49160 | tf_op jit(solution)/shard_map/ppermute | solution.py:11
  11.7 2.1 %all_to_all.8 = f32[128,2,512]{2,1,0:T(2,128)} reshape(f32[1,1,256,512]{3,2,1,0:T(8,128)} %param.18) | data formatting | bytes 1048576 | tf_op jit(solution)/shard_map/all_to_all | solution.py:68
  13.9 10.3 %all-to-all-start = ((f32[128,2,512]{2,1,0:T(2,128)}), f32[128,2,512]{2,1,0:T(2,128)S(1)}, u32[]{:S(2)}, u32[]{:S(2)}) async-start(f32[128,2,512]{2,1,0:T(2,128)} %all_to_all.8), calls=%async_computation | async-start | bytes 1048576 | tf_op jit(solution)/shard_map/all_to_all | solution.py:68
  24.1 0.0 copy-start.2
  24.2 1.7 %fusion.11 = f32[3,64,512]{2,1,0:T(8,128)S(1)} fusion(f32[3,64,256]{2,1,0:T(8,128)S(1)} %copy-done, f32[16,256,512]{2,1,0:T(8,128)} %param.12), kind=kOutput, calls=%fused_computation.15 | convolution fusion | flops 301989888 | bytes 1114112 | tf_op jit(solution)/shard_map/dot_general | solution.py:21
  25.9 2.8 %fusion.13 = f32[3,64,512]{2,1,0:T(8,128)} fusion(f32[3,64,256]{2,1,0:T(8,128)S(1)} %copy-done, f32[16,256,512]{2,1,0:T(8,128)} %param.12), kind=kOutput, calls=%fused_computation.17 | convolution fusion | flops 301989888 | bytes 1114112 | tf_op jit(solution)/shard_map/dot_general | solution.py:21
  28.6 2.3 %fusion.15 = f32[3,64,512]{2,1,0:T(8,128)} fusion(f32[3,64,256]{2,1,0:T(8,128)S(1)} %copy-done, f32[16,256,512]{2,1,0:T(8,128)} %param.12), kind=kOutput, calls=%fused_computation.19 | convolution fusion | flops 301989888 | bytes 1114112 | tf_op jit(solution)/shard_map/dot_general | solution.py:21
  30.9 2.3 %fusion.17 = f32[3,64,512]{2,1,0:T(8,128)} fusion(f32[3,64,256]{2,1,0:T(8,128)S(1)} %copy-done, f32[16,256,512]{2,1,0:T(8,128)} %param.12), kind=kOutput, calls=%fused_computation.21 | convolution fusion | flops 301989888 | bytes 1114112 | tf_op jit(solution)/shard_map/dot_general | solution.py:21
  33.2 2.3 %fusion.19 = f32[3,64,512]{2,1,0:T(8,128)} fusion(f32[3,64,256]{2,1,0:T(8,128)S(1)} %copy-done, f32[16,256,512]{2,1,0:T(8,128)} %param.12), kind=kOutput, calls=%fused_computation.23 | convolution fusion | flops 301989888 | bytes 1114112 | tf_op jit(solution)/shard_map/dot_general | solution.py:21
  35.6 2.3 %fusion.21 = f32[3,64,512]{2,1,0:T(8,128)} fusion(f32[3,64,256]{2,1,0:T(8,128)S(1)} %copy-done, f32[16,256,512]{2,1,0:T(8,128)} %param.12), kind=kOutput, calls=%fused_computation.25 | convolution fusion | flops 301989888 | bytes 1114112 | tf_op jit(solution)/shard_map/dot_general | solution.py:21
  37.9 2.3 %fusion.23 = f32[3,64,512]{2,1,0:T(8,128)} fusion(f32[3,64,256]{2,1,0:T(8,128)S(1)} %copy-done, f32[16,256,512]{2,1,0:T(8,128)} %param.12), kind=kOutput, calls=%fused_computation.27 | convolution fusion | flops 301989888 | bytes 1114112 | tf_op jit(solution)/shard_map/dot_general | solution.py:21
  40.2 2.3 %fusion.25 = f32[3,64,512]{2,1,0:T(8,128)} fusion(f32[3,64,256]{2,1,0:T(8,128)S(1)} %copy-done, f32[16,256,512]{2,1,0:T(8,128)} %param.12), kind=kOutput, calls=%fused_computation.29 | convolution fusion | flops 301989888 | bytes 1114112 | tf_op jit(solution)/shard_map/dot_general | solution.py:21
  42.5 1.3 %fusion.27 = f32[3,64,512]{2,1,0:T(8,128)} fusion(f32[3,64,256]{2,1,0:T(8,128)S(1)} %copy-done, f32[16,256,512]{2,1,0:T(8,128)S(1)} %copy-done.2), kind=kOutput, calls=%fused_computation.31 | convolution fusion | flops 301989888 | bytes 1114112 | tf_op jit(solution)/shard_map/dot_general | solution.py:21
  43.8 1.3 %fusion.29 = f32[3,64,512]{2,1,0:T(8,128)} fusion(f32[3,64,256]{2,1,0:T(8,128)S(1)} %copy-done, f32[16,256,512]{2,1,0:T(8,128)S(1)} %copy-done.2), kind=kOutput, calls=%fused_computation.33 | convolution fusion | flops 301989888 | bytes 1114112 | tf_op jit(solution)/shard_map/dot_general | solution.py:21
  45.1 1.3 %fusion.31 = f32[3,64,512]{2,1,0:T(8,128)} fusion(f32[3,64,256]{2,1,0:T(8,128)S(1)} %copy-done, f32[16,256,512]{2,1,0:T(8,128)S(1)} %copy-done.2), kind=kOutput, calls=%fused_computation.35 | convolution fusion | flops 301989888 | bytes 1114112 | tf_op jit(solution)/shard_map/dot_general | solution.py:21
  46.3 1.3 %fusion.33 = f32[3,64,512]{2,1,0:T(8,128)} fusion(f32[3,64,256]{2,1,0:T(8,128)S(1)} %copy-done, f32[16,256,512]{2,1,0:T(8,128)S(1)} %copy-done.2), kind=kOutput, calls=%fused_computation.37 | convolution fusion | flops 301989888 | bytes 1114112 | tf_op jit(solution)/shard_map/dot_general | solution.py:21
  47.6 1.3 %fusion.35 = f32[3,64,512]{2,1,0:T(8,128)} fusion(f32[3,64,256]{2,1,0:T(8,128)S(1)} %copy-done, f32[16,256,512]{2,1,0:T(8,128)S(1)} %copy-done.2), kind=kOutput, calls=%fused_computation.39 | convolution fusion | flops 301989888 | bytes 1114112 | tf_op jit(solution)/shard_map/dot_general | solution.py:21
  48.9 1.3 %fusion.37 = f32[3,64,512]{2,1,0:T(8,128)} fusion(f32[3,64,256]{2,1,0:T(8,128)S(1)} %copy-done, f32[16,256,512]{2,1,0:T(8,128)S(1)} %copy-done.2), kind=kOutput, calls=%fused_computation.41 | convolution fusion | flops 301989888 | bytes 1114112 | tf_op jit(solution)/shard_map/dot_general | solution.py:21
  50.2 1.3 %fusion.7 = f32[3,64,512]{2,1,0:T(8,128)} fusion(f32[3,64,256]{2,1,0:T(8,128)S(1)} %copy-done, f32[16,256,512]{2,1,0:T(8,128)S(1)} %copy-done.2), kind=kOutput, calls=%fused_computation.11 | convolution fusion | flops 301989888 | bytes 1114112 | tf_op jit(solution)/shard_map/dot_general | solution.py:21
  51.5 1.3 %fusion.9 = f32[3,64,512]{2,1,0:T(8,128)} fusion(f32[3,64,256]{2,1,0:T(8,128)S(1)} %copy-done, f32[16,256,512]{2,1,0:T(8,128)S(1)} %copy-done.2), kind=kOutput, calls=%fused_computation.13 | convolution fusion | flops 301989888 | bytes 1114112 | tf_op jit(solution)/shard_map/dot_general | solution.py:21
  52.8 2.8 %fusion.132 = (f32[8,128,511]{2,1,0:T(8,128)}, f32[8,128,511]{2,1,0:T(8,128)}) fusion(f32[8,128,512]{2,1,0:T(8,128)S(1)} %copy-done.1), kind=kLoop, calls=%fused_computation.182 | loop fusion | bytes 8372224 | tf_op jit(solution)/shard_map/slice | solution.py:77
  55.6 2.5 %fusion.134 = (f32[8,127,512]{2,1,0:T(8,128)}, f32[8,127,512]{2,1,0:T(8,128)}) fusion(f32[8,128,512]{2,1,0:T(8,128)S(1)} %copy-done.1), kind=kLoop, calls=%fused_computation.184 | loop fusion | bytes 8323072 | tf_op jit(solution)/shard_map/slice | solution.py:75
  58.0 2.4 %fusion.129 = (f32[7,128,512]{2,1,0:T(8,128)}, f32[7,128,512]{2,1,0:T(8,128)}) fusion(f32[8,128,512]{2,1,0:T(8,128)S(1)} %copy-done.1), kind=kLoop, calls=%fused_computation.179 | loop fusion | bytes 7340032 | tf_op jit(solution)/shard_map/slice | solution.py:81
  60.4 0.7 fusion.130
  61.1 0.7 fusion.112
  61.8 0.1 mul.546
  61.9 0.8 mul.550
  62.7 1.4 %mul.554 = f32[64,2]{1,0:T(8,128)} reshape(f32[128]{0:T(128)} %get-tuple-element.26) | data formatting | bytes 1024 | tf_op jit(solution)/shard_map/mul | solution.py:22
  64.1 1.3 %mul.558 = f32[64,2]{1,0:T(8,128)} reshape(f32[128]{0:T(128)} %get-tuple-element.25) | data formatting | bytes 1024 | tf_op jit(solution)/shard_map/mul | solution.py:22
  65.5 1.3 %mul.562 = f32[64,2]{1,0:T(8,128)} reshape(f32[128]{0:T(128)} %get-tuple-element.24) | data formatting | bytes 1024 | tf_op jit(solution)/shard_map/mul | solution.py:22
  66.8 1.4 %mul.566 = f32[64,2]{1,0:T(8,128)} reshape(f32[128]{0:T(128)} %get-tuple-element.23) | data formatting | bytes 1024 | tf_op jit(solution)/shard_map/mul | solution.py:22
  68.2 1.3 %mul.570 = f32[64,2]{1,0:T(8,128)} reshape(f32[128]{0:T(128)} %get-tuple-element.22) | data formatting | bytes 1024 | tf_op jit(solution)/shard_map/mul | solution.py:22
  69.5 1.3 %mul.574 = f32[64,2]{1,0:T(8,128)} reshape(f32[128]{0:T(128)} %get-tuple-element.21) | data formatting | bytes 1024 | tf_op jit(solution)/shard_map/mul | solution.py:22
  70.8 1.3 %mul.578 = f32[64,2]{1,0:T(8,128)} reshape(f32[128]{0:T(128)} %get-tuple-element.20) | data formatting | bytes 1024 | tf_op jit(solution)/shard_map/mul | solution.py:22
  72.2 1.3 %mul.582 = f32[64,2]{1,0:T(8,128)} reshape(f32[128]{0:T(128)} %get-tuple-element.19) | data formatting | bytes 1024 | tf_op jit(solution)/shard_map/mul | solution.py:22
  73.5 1.4 %mul.586 = f32[64,2]{1,0:T(8,128)} reshape(f32[128]{0:T(128)} %get-tuple-element.18) | data formatting | bytes 1024 | tf_op jit(solution)/shard_map/mul | solution.py:22
  74.9 1.3 %mul.590 = f32[64,2]{1,0:T(8,128)} reshape(f32[128]{0:T(128)} %get-tuple-element.17) | data formatting | bytes 1024 | tf_op jit(solution)/shard_map/mul | solution.py:22
  76.3 1.4 %mul.594 = f32[64,2]{1,0:T(8,128)} reshape(f32[128]{0:T(128)} %get-tuple-element.16) | data formatting | bytes 1024 | tf_op jit(solution)/shard_map/mul | solution.py:22
  77.7 1.4 %mul.598 = f32[64,2]{1,0:T(8,128)} reshape(f32[128]{0:T(128)} %get-tuple-element.15) | data formatting | bytes 1024 | tf_op jit(solution)/shard_map/mul | solution.py:22
  79.0 1.4 %mul.602 = f32[64,2]{1,0:T(8,128)} reshape(f32[128]{0:T(128)} %get-tuple-element.29) | data formatting | bytes 1024 | tf_op jit(solution)/shard_map/mul | solution.py:22
  80.4 1.4 %mul.606 = f32[64,2]{1,0:T(8,128)} reshape(f32[128]{0:T(128)} %get-tuple-element.28) | data formatting | bytes 1024 | tf_op jit(solution)/shard_map/mul | solution.py:22
  81.8 6.2 %multiply_add_fusion = f32[3,64,2,512]{3,2,1,0:T(2,128)S(1)} fusion(f32[3,64,512]{2,1,0:T(8,128)} %fusion.7, f32[64,2]{1,0:T(8,128)} %mul.606, f32[3,64,512]{2,1,0:T(8,128)} %fusion.9, f32[64,2]{1,0:T(8,128)} %mul.602, f32[3,64,512]{2,1,0:T(8,128)S(1)} %fusion.11, f32[64,2]{1,0:T(8,128)} %mul.598, f32[3,64,512]{2,1,0:T(8,128)} %fusion.13, f32[64,2]{1,0:T(8,128)} %mul.594, ...), kind=kLoop, calls=%fused_computation.10 | loop fusion | flops 6094848 | bytes 7086080 | tf_op jit(solution)/shard_map/add | solution.py:22
  88.1 1.3 %fusion.56 = (f32[1,64,2,512]{3,2,1,0:T(2,128)}, f32[1,64,2,512]{3,2,1,0:T(2,128)}, f32[1,64,2,512]{3,2,1,0:T(2,128)}) fusion(f32[3,64,2,512]{3,2,1,0:T(2,128)S(1)} %multiply_add_fusion), kind=kLoop, calls=%fused_computation.63 | loop fusion | flops 327680 | bytes 1572864 | tf_op jit(solution)/shard_map/add | solution.py:38
  89.4 0.7 fusion.135
  90.1 0.2 convert_reduce_fusion
  90.3 0.6 slice.229
  90.9 1.8 %add.257 = f32[128,512]{1,0:T(8,128)} reshape(f32[1,64,2,512]{3,2,1,0:T(2,128)} %get-tuple-element.47) | data formatting | bytes 524288 | tf_op jit(solution)/shard_map/add | solution.py:38
  92.8 1.8 %add.265 = f32[128,512]{1,0:T(8,128)} reshape(f32[1,64,2,512]{3,2,1,0:T(2,128)} %get-tuple-element.49) | data formatting | bytes 524288 | tf_op jit(solution)/shard_map/add | solution.py:36
  94.6 1.8 %mul.626 = f32[128,512]{1,0:T(8,128)} reshape(f32[1,64,2,512]{3,2,1,0:T(2,128)} %get-tuple-element.48) | data formatting | bytes 524288 | tf_op jit(solution)/shard_map/mul | solution.py:37
  96.5 6.8 %fusion.5 = f32[8,128,512]{2,1,0:T(8,128)S(1)} fusion(f32[8,128,512]{2,1,0:T(8,128)S(1)} %copy-done.1, f32[8,1,512]{2,1,0:T(1,128)S(1)} %collective-permute-done, f32[8,127,512]{2,1,0:T(8,128)} %get-tuple-element.46, f32[8,127,512]{2,1,0:T(8,128)} %get-tuple-element.45, f32[8,1,512]{2,1,0:T(1,128)} %collective-permute-done.1, ...), kind=kLoop, calls=%fused_computation.7 | loop fusion | flops 9437184 | bytes 18874368 | tf_op jit(solution)/shard_map/add | solution.py:83
  103.3 0.0 copy-start.3
  103.3 1.3 %copy-done.3 = f32[8,128,512]{2,1,0:T(8,128)} copy-done((f32[8,128,512]{2,1,0:T(8,128)}, f32[8,128,512]{2,1,0:T(8,128)S(1)}, u32[]{:S(2)}) %copy-start.3) | copy-done | bytes 2097176
  104.7 0.4 all_to_all.10
  105.0 0.0 slice-start
  105.0 0.8 gather_fusion
  105.8 15.6 %fusion.99 = (f32[128,512]{1,0:T(8,128)S(1)}, pred[128,512]{1,0:T(8,128)(4,1)S(1)}, pred[128,512]{1,0:T(8,128)(4,1)S(1)}, pred[128,512]{1,0:T(8,128)(4,1)S(1)}, pred[128,512]{1,0:T(8,128)(4,1)S(1)}) fusion(f32[128,512]{1,0:T(8,128)S(1)} %copy-done.8, f32[128,512]{1,0:T(8,128)S(1)} %copy-done.9, f32[128,512]{1,0:T(8,128)S(1)} %gather_fusion, ...), kind=kLoop, calls=%fused_computation.120 | loop fusion | flops 12648448 | bytes 2097232 | tf_op jit(solution)/shard_map/add | solution.py:52
  121.4 0.0 copy-start.10
  121.5 2.8 %fusion.57 = f32[8,128,512]{2,1,0:T(8,128)S(1)} fusion(f32[8,128,512]{2,1,0:T(8,128)S(1)} %copy-done.4, f32[1,128,512]{2,1,0:T(8,128)S(1)} %slice-done, f32[128,512]{1,0:T(8,128)S(1)} %get-tuple-element.30, pred[128,512]{1,0:T(8,128)(4,1)S(1)} %get-tuple-element.34, pred[128,512]{1,0:T(8,128)(4,1)S(1)} %get-tuple-element.33, ...), kind=kLoop, calls=%fused_computation.65 | loop fusion | flops 720896 | bytes 1048592 | tf_op jit(solution)/shard_map/scatter-add | solution.py:93
  124.3 1.3 %copy-done.5 = f32[8,128,512]{2,1,0:T(8,128)} copy-done((f32[8,128,512]{2,1,0:T(8,128)}, f32[8,128,512]{2,1,0:T(8,128)S(1)}, u32[]{:S(2)}) %copy-start.5) | copy-done | bytes 2097176
  (33 shorter events, 0.1 us)
Async XLA Ops:
  0.6 23.5 %copy-start = (f32[3,64,256]{2,1,0:T(8,128)S(1)}, f32[3,64,256]{2,1,0:T(8,128)}, u32[]{:S(2)}) copy-start(f32[3,64,256]{2,1,0:T(8,128)} %param.11) | copy-start | bytes 589828
  0.6 5.5 %copy-start.1 = (f32[8,128,512]{2,1,0:T(8,128)S(1)}, f32[8,128,512]{2,1,0:T(8,128)}, u32[]{:S(2)}) copy-start(f32[8,128,512]{2,1,0:T(8,128)} %param.16) | copy-start | bytes 6291460
  3.1 93.3 %collective-permute-start.2 = (f32[8,128,1]{2,1,0:T(8,128)}, f32[8,128,1]{2,1,0:T(8,128)}, u32[]{:S(2)}, u32[]{:S(2)}) collective-permute-start(f32[8,128,1]{2,1,0:T(8,128)} %get-tuple-element.40), channel_id=1, source_target_pairs={{0,112},{16,0},{32,16},{48,32},{64,48},{80,64},{96,80},{112,96},{1... | collective-permute-start | bytes 12296 | tf_op jit(solution)/shard_map/ppermute | solution.py:11
  4.5 91.9 %collective-permute-start.3 = (f32[8,128,1]{2,1,0:T(8,128)}, f32[8,128,1]{2,1,0:T(8,128)}, u32[]{:S(2)}, u32[]{:S(2)}) collective-permute-start(f32[8,128,1]{2,1,0:T(8,128)} %get-tuple-element.39), channel_id=1, source_target_pairs={{0,16},{16,32},{32,48},{48,64},{64,80},{80,96},{96,112},{112,0},{1... | collective-permute-start | bytes 12296 | tf_op jit(solution)/shard_map/ppermute | solution.py:11
  6.8 89.7 %collective-permute-start = (f32[8,1,512]{2,1,0:T(1,128)}, f32[8,1,512]{2,1,0:T(1,128)S(1)}, u32[]{:S(2)}, u32[]{:S(2)}) collective-permute-start(f32[8,1,512]{2,1,0:T(1,128)} %get-tuple-element.44), channel_id=1, source_target_pairs={{0,15},{1,0},{2,1},{3,2},{4,3},{5,4},{6,5},{7,6},{8,7},{9,8},{10,9... | collective-permute-start | bytes 49160 | tf_op jit(solution)/shard_map/ppermute | solution.py:11
  11.7 84.7 %collective-permute-start.1 = (f32[8,1,512]{2,1,0:T(1,128)}, f32[8,1,512]{2,1,0:T(1,128)}, u32[]{:S(2)}, u32[]{:S(2)}) collective-permute-start(f32[8,1,512]{2,1,0:T(1,128)} %get-tuple-element.43), channel_id=1, source_target_pairs={{0,1},{1,2},{2,3},{3,4},{4,5},{5,6},{6,7},{7,8},{8,9},{9,10},{10,1... | collective-permute-start | bytes 49160 | tf_op jit(solution)/shard_map/ppermute | solution.py:11
  13.9 90.8 %all-to-all-start = ((f32[128,2,512]{2,1,0:T(2,128)}), f32[128,2,512]{2,1,0:T(2,128)S(1)}, u32[]{:S(2)}, u32[]{:S(2)}) async-start(f32[128,2,512]{2,1,0:T(2,128)} %all_to_all.8), calls=%async_computation | async-start | bytes 1048576 | tf_op jit(solution)/shard_map/all_to_all | solution.py:68
  24.1 18.4 %copy-start.2 = (f32[16,256,512]{2,1,0:T(8,128)S(1)}, f32[16,256,512]{2,1,0:T(8,128)}, u32[]{:S(2)}) copy-start(f32[16,256,512]{2,1,0:T(8,128)} %param.12) | copy-start | bytes 25165828
  58.0 3.1 %copy-start.13 = (s32[1,128,2]{1,2,0:T(2,128)S(1)}, s32[1,128,2]{1,2,0:T(2,128)}, u32[]{:S(2)}) copy-start(s32[1,128,2]{1,2,0:T(2,128)} %param.13) | copy-start | bytes 3076
  81.8 7.5 %copy-start.12 = (f32[5,4]{0,1:T(4,128)S(1)}, f32[5,4]{0,1:T(4,128)}, u32[]{:S(2)}) copy-start(f32[5,4]{0,1:T(4,128)} %param.19) | copy-start | bytes 244
  81.8 8.3 %copy-start.14 = (s32[1,128,1]{1,2,0:T(1,128)S(1)}, s32[1,128,1]{1,2,0:T(1,128)}, u32[]{:S(2)}) copy-start(s32[1,128,1]{1,2,0:T(1,128)} %param.14) | copy-start | bytes 1540
  88.1 8.4 %copy-start.6 = (f32[1,128,512]{2,1,0:T(8,128)S(1)}, f32[1,128,512]{2,1,0:T(8,128)}, u32[]{:S(2)}) copy-start(f32[1,128,512]{2,1,0:T(8,128)} %get-tuple-element.38) | copy-start | bytes 786436
  103.3 1.3 %copy-start.3 = (f32[8,128,512]{2,1,0:T(8,128)}, f32[8,128,512]{2,1,0:T(8,128)S(1)}, u32[]{:S(2)}) copy-start(f32[8,128,512]{2,1,0:T(8,128)S(1)} %fusion.5) | copy-start | bytes 6291460
  104.6 1.2 copy-start.7
  104.6 1.2 copy-start.8
  104.6 1.2 copy-start.9
  104.6 1.2 copy-start.11
  105.0 16.4 %slice-start = ((f32[8,128,512]{2,1,0:T(8,128)}), f32[1,128,512]{2,1,0:T(8,128)S(1)}, s32[]{:S(2)}) async-start(f32[8,128,512]{2,1,0:T(8,128)} %copy-done.3), calls=%async_computation.1 | async-start | bytes 524288 | tf_op jit(solution)/shard_map/slice | solution.py:92
  105.8 15.7 %copy-start.4 = (f32[8,128,512]{2,1,0:T(8,128)S(1)}, f32[8,128,512]{2,1,0:T(8,128)}, u32[]{:S(2)}) copy-start(f32[8,128,512]{2,1,0:T(8,128)} %copy-done.3) | copy-start | bytes 6291460
  121.4 2.8 %copy-start.10 = (f32[128,512]{1,0:T(8,128)}, f32[128,512]{1,0:T(8,128)S(1)}, u32[]{:S(2)}) copy-start(f32[128,512]{1,0:T(8,128)S(1)} %get-tuple-element.30) | copy-start | bytes 786436
  124.2 1.3 %copy-start.5 = (f32[8,128,512]{2,1,0:T(8,128)}, f32[8,128,512]{2,1,0:T(8,128)S(1)}, u32[]{:S(2)}) copy-start(f32[8,128,512]{2,1,0:T(8,128)S(1)} %fusion.57) | copy-start | bytes 6291460

commit v2 on v1

v2 whole, which is shorter than its diff:
```python
import jax
import jax.numpy as jnp
from jax import lax
from jax.experimental import pallas as pl
from jax.experimental.pallas import tpu as pltpu
from jax.sharding import PartitionSpec as P

NEWTON = 6
MESH = pl.DeviceIdType.MESH
LANES = 128
EARLY_TILES = 5
STRIP = 16


def split_two(values):
    high = values.astype(jnp.bfloat16)
    low = (values - high.astype(jnp.float32)).astype(jnp.bfloat16)
    return high, low


def make_kernel(n_gx, n_gy, layers, rows, cols, tiles, half):
    devices = n_gx * n_gy
    pairs = rows // 2
    blocks = cols // LANES

    def kernel(
        panels_ref, uses_ref, owner_ref, table_ref,
        soil_hbm, substrate_hbm, conductivity_hbm, kinds_hbm, tiles_hbm,
        skin_hbm, out_hbm,
        soil, send, recv, substrate, conductivity, kinds, weights, coarse, flux,
        diffused, skin, wet,
        send_n, send_s, send_w, send_e, north, south, west, east,
        load_sem, tile_sem, out_sem, a2a_send, a2a_recv, halo_send, halo_recv, own_sem,
    ):
        gx = lax.axis_index("gx")
        gy = lax.axis_index("gy")
        me = gx * n_gy + gy

        loads = [
            pltpu.make_async_copy(soil_hbm, soil, load_sem.at[0]),
            pltpu.make_async_copy(substrate_hbm, substrate, load_sem.at[1]),
            pltpu.make_async_copy(conductivity_hbm, conductivity, load_sem.at[2]),
            pltpu.make_async_copy(kinds_hbm, kinds, load_sem.at[3]),
        ]

        def tile_copy(pick):
            return pltpu.make_async_copy(tiles_hbm.at[pick], weights.at[pick], tile_sem.at[pick])

        loads[0].start()
        loads[1].start()
        for pick in range(tiles):
            tile_copy(pick).start()
        loads[2].start()
        loads[3].start()

        barrier = pltpu.get_barrier_semaphore()

        def greet(offset, carry):
            other = lax.rem(me + offset, devices)
            pl.semaphore_signal(
                barrier, inc=1, device_id=(other // n_gy, lax.rem(other, n_gy)), device_id_type=MESH
            )
            return carry

        lax.fori_loop(1, devices, greet, 0)

        flat = panels_ref[...].reshape(3 * pairs, half)
        high, low = split_two(flat)
        coarse[pl.ds(0, 3 * pairs), :] = high
        coarse[pl.ds(3 * pairs, 3 * pairs), :] = low
        flux[...] = jnp.zeros_like(flux)

        loads[0].wait()
        for block in range(blocks):
            send[pl.ds(block, devices * 2, stride=blocks), :] = soil[:, block * LANES : (block + 1) * LANES]

        loads[1].wait()
        lane = lax.broadcasted_iota(jnp.int32, (rows, LANES), 1)
        gather_w = jnp.zeros((rows, LANES), jnp.float32)
        gather_e = jnp.zeros((rows, LANES), jnp.float32)
        for layer in range(layers):
            send_n[layer : layer + 1, :] = substrate[layer, 0:1, :]
            send_s[layer : layer + 1, :] = substrate[layer, rows - 1 : rows, :]
            left = substrate[layer, :, 0:LANES]
            right = substrate[layer, :, cols - LANES : cols]
            gather_w = jnp.where(lane == layer, left[:, 0:1], gather_w)
            gather_e = jnp.where(lane == layer, right[:, LANES - 1 : LANES], gather_e)
        send_w[...] = gather_w.T[0:layers, :]
        send_e[...] = gather_e.T[0:layers, :]

        def regrid_tile(pick, carry):
            tile_copy(pick).wait()
            uses = [
                sum(
                    jnp.where(uses_ref[pl.ds(parity, pairs, stride=2), :][:, k : k + 1] == pick, 1.0, 0.0)
                    for k in range(2)
                )
                for parity in range(2)
            ]
            for column in range(0, cols, 256):
                w_high, w_low = split_two(weights[pick, :, column : column + 256])
                both = jnp.dot(coarse[...], w_high, preferred_element_type=jnp.float32)
                cross = jnp.dot(
                    coarse[pl.ds(0, 3 * pairs), :], w_low, preferred_element_type=jnp.float32
                )
                product = both[: 3 * pairs] + both[3 * pairs :] + cross
                for field in range(3):
                    part = product[field * pairs : (field + 1) * pairs]
                    for parity in range(2):
                        flux[field, parity, :, column : column + 256] += uses[parity] * part
            return carry

        lax.fori_loop(0, EARLY_TILES, regrid_tile, 0)

        pl.semaphore_wait(barrier, devices - 1)

        def halo_copy(source, target, slot, device_id):
            return pltpu.make_async_remote_copy(
                src_ref=source, dst_ref=target, send_sem=halo_send.at[slot],
                recv_sem=halo_recv.at[slot], device_id=device_id, device_id_type=MESH,
            )

        up = lax.rem(gy + n_gy - 1, n_gy)
        down = lax.rem(gy + 1, n_gy)
        before = lax.rem(gx + n_gx - 1, n_gx)
        after = lax.rem(gx + 1, n_gx)
        halos = [
            halo_copy(send_n, south, 0, (gx, up)),
            halo_copy(send_s, north, 1, (gx, down)),
            halo_copy(send_w, east, 2, (before, gy)),
            halo_copy(send_e, west, 3, (after, gy)),
        ]
        for copy in halos:
            copy.start()

        def hand(offset, carry):
            other = lax.rem(me + offset, devices)
            pltpu.make_async_remote_copy(
                src_ref=send.at[pl.ds(pl.multiple_of(other * 8, 8), 8), :],
                dst_ref=recv.at[pl.ds(pl.multiple_of(me * 8, 8), 8), :],
                send_sem=a2a_send, recv_sem=a2a_recv,
                device_id=(other // n_gy, lax.rem(other, n_gy)), device_id_type=MESH,
            ).start()
            return carry

        lax.fori_loop(1, devices, hand, 0)
        own = pltpu.make_async_copy(
            send.at[pl.ds(pl.multiple_of(me * 8, 8), 8), :],
            recv.at[pl.ds(pl.multiple_of(me * 8, 8), 8), :],
            own_sem,
        )
        own.start()

        lax.fori_loop(EARLY_TILES, tiles, regrid_tile, 0)

        owner_wide = jnp.broadcast_to(owner_ref[...], (rows, rows))
        owner_tall = owner_wide.T
        row_id = lax.broadcasted_iota(jnp.int32, (rows, rows), 0)
        col_id = lax.broadcasted_iota(jnp.int32, (rows, rows), 1)
        twin = jnp.where((owner_wide == owner_tall) & (col_id < row_id), 1.0, 0.0)
        second = jnp.sum(twin, axis=1, keepdims=True) > 0.5
        named = jnp.where(owner_tall == col_id, 1.0, 0.0)
        first_hot = jnp.where(second, 0.0, named).astype(jnp.bfloat16)
        second_hot = jnp.where(second, named, 0.0).astype(jnp.bfloat16)
        hot = jnp.concatenate([first_hot, second_hot], axis=1)

        loads[2].wait()
        loads[3].wait()
        for copy in halos:
            copy.wait()
        west_tall = west[...].T
        east_tall = east[...].T
        strip_row = lax.broadcasted_iota(jnp.int32, (STRIP, cols), 0)
        strip_col = lax.broadcasted_iota(jnp.int32, (STRIP, cols), 1)
        for layer in range(layers):
            for base in range(0, rows, STRIP):
                here = substrate[layer, base : base + STRIP, :]
                if base:
                    row_up = substrate[layer, base - 1 : base, :]
                else:
                    row_up = north[layer : layer + 1, :]
                if base + STRIP < rows:
                    row_down = substrate[layer, base + STRIP : base + STRIP + 1, :]
                else:
                    row_down = south[layer : layer + 1, :]
                lateral = jnp.where(strip_row == 0, row_up, pltpu.roll(here, 1, 0))
                lateral += jnp.where(strip_row == STRIP - 1, row_down, pltpu.roll(here, STRIP - 1, 0))
                lateral += jnp.where(
                    strip_col == 0, west_tall[base : base + STRIP, layer : layer + 1], pltpu.roll(here, 1, 1)
                )
                lateral += jnp.where(
                    strip_col == cols - 1,
                    east_tall[base : base + STRIP, layer : layer + 1],
                    pltpu.roll(here, cols - 1, 1),
                )
                above = substrate[max(layer - 1, 0), base : base + STRIP, :]
                below = substrate[min(layer + 1, layers - 1), base : base + STRIP, :]
                change = (lateral - 4.0 * here) + (above + below - 2.0 * here)
                diffused[layer, base : base + STRIP, :] = (
                    here + 0.08 * conductivity[layer, base : base + STRIP, :] * change
                )
        outs = [
            pltpu.make_async_copy(
                diffused.at[pl.ds(1, layers - 1)], out_hbm.at[pl.ds(1, layers - 1)], out_sem.at[0]
            ),
            pltpu.make_async_copy(diffused.at[0], out_hbm.at[0], out_sem.at[1]),
            pltpu.make_async_copy(skin, skin_hbm, out_sem.at[2]),
        ]
        outs[0].start()

        own.wait()
        everything = pltpu.make_async_remote_copy(
            src_ref=send.at[pl.ds(0, (devices - 1) * 8), :],
            dst_ref=recv.at[pl.ds(0, (devices - 1) * 8), :],
            send_sem=a2a_send, recv_sem=a2a_recv, device_id=(gx, down), device_id_type=MESH,
        )
        everything.wait_recv()
        for block in range(blocks):
            taken = jnp.concatenate(
                [recv[pl.ds(block, devices, stride=8), :], recv[pl.ds(blocks + block, devices, stride=8), :]],
                axis=0,
            )
            t_high, t_low = split_two(taken)
            wet[:, block * LANES : (block + 1) * LANES] = jnp.dot(
                hot, t_high, preferred_element_type=jnp.float32
            ) + jnp.dot(hot, t_low, preferred_element_type=jnp.float32)

        def strip(index, carry):
            base = pl.multiple_of(index * STRIP, STRIP)
            spot = pl.ds(base, STRIP)
            kind = kinds[spot, :]
            is0, is1, is2 = kind == 0, kind == 1, kind == 2

            def lookup(row):
                return jnp.where(
                    is0, table_ref[row, 0],
                    jnp.where(is1, table_ref[row, 1], jnp.where(is2, table_ref[row, 2], table_ref[row, 3])),
                )

            pair = pl.ds(pl.multiple_of(index * (STRIP // 2), STRIP // 2), STRIP // 2)

            def fine(field):
                even = flux[field, 0, pair, :]
                odd = flux[field, 1, pair, :]
                return jnp.stack([even, odd], axis=1).reshape(STRIP, cols)

            absorb, emit, sensible, beta, conduct = [lookup(row) for row in range(5)]
            top = diffused[0, spot, :]
            wetness = beta * wet[spot, :]
            fixed = (
                absorb * (2.0 + 0.3 * fine(2))
                + sensible * (1.0 + 0.2 * fine(0))
                + wetness * (0.2 * fine(1))
                + conduct * top
            )
            linear = sensible + conduct
            temp = top
            for _ in range(NEWTON):
                moisture = wetness * jnp.exp(1.5 * (temp - 1.0))
                size = jnp.abs(temp)
                cube = emit * (size * size * size)
                residual = fixed - temp * (cube + linear) - moisture
                slope = 4.0 * cube + linear + 1.5 * moisture
                temp = temp + 0.4 * residual / slope
            skin[spot, :] = temp
            diffused[0, spot, :] = top + 0.5 * (conduct * (temp - top))
            return carry

        lax.fori_loop(0, rows // STRIP, strip, 0)
        outs[1].start()
        outs[2].start()
        everything.wait_send()
        for copy in outs:
            copy.wait()

    return kernel


def per_device(
    panels,
    regrid_tiles,
    weight_index,
    owner,
    surface_type,
    substrate,
    conductivity,
    soil_wetness,
    surface_table,
):
    n_gx, n_gy = lax.axis_size("gx"), lax.axis_size("gy")
    devices = n_gx * n_gy
    layers, rows, cols = substrate.shape
    tiles, half, _ = regrid_tiles.shape
    f32 = jnp.float32
    vmem = pl.BlockSpec(memory_space=pltpu.VMEM)
    hbm = pl.BlockSpec(memory_space=pl.ANY)
    return pl.pallas_call(
        make_kernel(n_gx, n_gy, layers, rows, cols, tiles, half),
        out_shape=(
            jax.ShapeDtypeStruct((rows, cols), f32),
            jax.ShapeDtypeStruct((layers, rows, cols), f32),
        ),
        in_specs=[vmem, vmem, vmem, pl.BlockSpec(memory_space=pltpu.SMEM)] + [hbm] * 5,
        out_specs=(hbm, hbm),
        scratch_shapes=[
            pltpu.VMEM((2 * devices, cols), f32),
            pltpu.VMEM((8 * devices, LANES), f32),
            pltpu.VMEM((8 * devices, LANES), f32),
            pltpu.VMEM((layers, rows, cols), f32),
            pltpu.VMEM((layers, rows, cols), f32),
            pltpu.VMEM((rows, cols), jnp.int32),
            pltpu.VMEM((tiles, half, cols), f32),
            pltpu.VMEM((3 * rows, half), jnp.bfloat16),
            pltpu.VMEM((3, 2, rows // 2, cols), f32),
            pltpu.VMEM((layers, rows, cols), f32),
            pltpu.VMEM((rows, cols), f32),
            pltpu.VMEM((rows, cols), f32),
            pltpu.VMEM((layers, cols), f32),
            pltpu.VMEM((layers, cols), f32),
            pltpu.VMEM((layers, rows), f32),
            pltpu.VMEM((layers, rows), f32),
            pltpu.VMEM((layers, cols), f32),
            pltpu.VMEM((layers, cols), f32),
            pltpu.VMEM((layers, rows), f32),
            pltpu.VMEM((layers, rows), f32),
            pltpu.SemaphoreType.DMA((4,)),
            pltpu.SemaphoreType.DMA((tiles,)),
            pltpu.SemaphoreType.DMA((3,)),
            pltpu.SemaphoreType.DMA,
            pltpu.SemaphoreType.DMA,
            pltpu.SemaphoreType.DMA((4,)),
            pltpu.SemaphoreType.DMA((4,)),
            pltpu.SemaphoreType.DMA,
        ],
        compiler_params=pltpu.CompilerParams(
            collective_id=0, has_side_effects=True, vmem_limit_bytes=48 * 1024 * 1024
        ),
        name="surface_step",
    )(
        panels, weight_index[0], owner[0].reshape(1, rows), surface_table,
        soil_wetness[0, 0], substrate, conductivity, surface_type, regrid_tiles,
    )


def solution(mesh):
    placed = (
        P(None, "gy", "gx"),
        P(),
        P("gx", "gy", None),
        P("gx", "gy", None),
        P("gy", "gx"),
        P(None, "gy", "gx"),
        P(None, "gy", "gx"),
        P("gx", "gy", None, None),
        P(),
    )
    return jax.shard_map(
        per_device,
        mesh=mesh,
        in_specs=placed,
        out_specs=(P("gy", "gx"), P(None, "gy", "gx")),
        check_vma=False,
    )
```

time: 127 us -> 34.6 us (0.27)
  local copies, waits for them, and re-layouts: 44.3 us -> 8.73 us
  other arithmetic: 33.5 us -> 0 us
  matrix products: 28.6 us -> 0 us
  Pallas kernels: 0 us -> 24.9 us
  starting transfers between devices: 18.2 us -> 0 us
    add x4 -> x0, other arithmetic: 29.9 us -> none  [the longest x1 15.6 us: balance(): skin_temp = skin_temp + 0.4 * residual_f / slope_sum]
    dot_general x16 -> x0, matrix products: 28.6 us -> none  [regrid(): product = jnp.dot(flat, tables[pick], precision=lax.Precision.HIGHEST)]
    pallas_call x0 -> x1, Pallas kernels: none -> 24.9 us  [per_device(): pl.pallas_call(make_kernel(n_gx, n_gy, layers, rows, cols, tiles, half),...]
    mul x17 -> x0, local copies, waits for them, and re-layouts: 21.9 us -> none  [the longest x16 20 us: regrid(): total = total + uses * product.reshape(fields, coarse_rows, 1, width)]
    slice x10 -> x0, local copies, waits for them, and re-layouts: 12.8 us -> none  [the longest x2 3.09 us: per_device(): layer_below = jnp.concatenate([substrate[1:], substrate[-1:]], axis=0)]
    all_to_all x1 -> x0, starting transfers between devices: 10.3 us -> none  [per_device(): lax.all_to_all(soil_wetness[0, 0], ('gx', 'gy'), split_axis=0, concat_axi...]
    ppermute x4 -> x0, starting transfers between devices: 7.96 us -> none  [halo(): lax.ppermute(edge, axis, [(i, (i + step) % count) for i in range(count)])]
    unnamed x30 -> x14, local copies, waits for them, and re-layouts: 2.69 us -> 8.73 us
  transfers between devices with their start and end apart: 5 -> 0, of which waited for: 0 -> 0; matrix products, arithmetic and copies ran while one was open for 63% -> 0% of each run, Pallas kernels for 0% -> 0%
where the time goes in v2:
time: 34.6 us; the launch traced here: 34.3 us
  Pallas kernels  24.9 us (72%)
  local copies, waits for them, and re-layouts  8.73 us (25%)
  between operations  0.65 us (2%)
    pallas_call x1, Pallas kernels, per_device(): pl.pallas_call(make_kernel(n_gx, n_gy, layers, rows, cols, tiles, half),...  24.9 us
    unnamed x14, local copies, waits for them, and re-layouts  8.73 us

profile of v2, /device:TPU:1, one launch (start us, length us, event | category | flops | bytes accessed | tf_op | source)
XLA Modules:
  0.0 34.3 jit_solution(13117694600959602827)
XLA Ops:
  0.6 0.8 %copy.12.table_ref = f32[5,4]{1,0:T(8,128)S(1)} copy(f32[5,4]{0,1:T(4,128)} %param.17) | data formatting | bytes 160 | tf_op args[8]
  1.4 0.8 %copy.11 = s32[1,128,2]{2,1,0:T(8,128)S(1)} copy(s32[1,128,2]{1,2,0:T(2,128)} %param.11) | data formatting | bytes 2048 | tf_op args[2]
  2.2 0.0 copy-start
  2.2 1.6 %copy-done = f32[8,128,512]{2,1,0:T(8,128)S(1)} copy-done((f32[8,128,512]{2,1,0:T(8,128)S(1)}, f32[8,128,512]{2,1,0:T(8,128)}, u32[]{:S(2)}) %copy-start) | copy-done | bytes 2097176
  3.8 0.0 copy-start.1
  3.8 1.0 %copy-done.1 = f32[1,1,256,512]{3,2,1,0:T(8,128)S(1)} copy-done((f32[1,1,256,512]{3,2,1,0:T(8,128)S(1)}, f32[1,1,256,512]{3,2,1,0:T(8,128)}, u32[]{:S(2)}) %copy-start.1) | copy-done | bytes 524312
  4.8 0.0 copy-start.2
  4.8 0.9 %copy-done.2 = s32[128,512]{1,0:T(8,128)S(1)} copy-done((s32[128,512]{1,0:T(8,128)S(1)}, s32[128,512]{1,0:T(8,128)}, u32[]{:S(2)}) %copy-start.2) | copy-done | bytes 262168
  5.8 0.0 copy-start.3
  5.8 0.9 %copy-done.3 = f32[3,64,256]{2,1,0:T(8,128)S(1)} copy-done((f32[3,64,256]{2,1,0:T(8,128)S(1)}, f32[3,64,256]{2,1,0:T(8,128)}, u32[]{:S(2)}) %copy-start.3) | copy-done | bytes 196632
  6.7 0.0 copy-start.4
  6.7 0.7 %copy-done.4 = s32[1,128,1]{1,2,0:T(1,128)S(1)} copy-done((s32[1,128,1]{1,2,0:T(1,128)S(1)}, s32[1,128,1]{1,2,0:T(1,128)}, u32[]{:S(2)}) %copy-start.4) | copy-done | bytes 536
  7.3 24.9 %surface_step.1 = (f32[128,512]{1,0:T(8,128)S(1)}, f32[8,128,512]{2,1,0:T(8,128)S(1)}) custom-call(f32[3,64,256]{2,1,0:T(8,128)S(1)} %copy-done.3, s32[128,2]{1,0:T(8,128)S(1)} %bitcast.4, s32[1,128]{1,0:T(1,128)S(1)} %bitcast.5, f32[5,4]{1,0:T(8,128)S(1)} %copy.12.table_ref, f32[256,512]{1,0:T(8,128)S(1)} %bitcast.3, f32[8,128,512]{2,1,0:T(8,128)S(1)} %copy-done, ...), custom_call_target="tpu_custom_call" | custom-call | tf_op jit(solution)/shard_map/surface_step/pallas_call | solution.py:297
  32.2 0.7 %copy.15 = f32[128,512]{1,0:T(8,128)} copy(f32[128,512]{1,0:T(8,128)S(1)} %get-tuple-element.4) | data formatting | bytes 524288
  32.9 1.3 %copy.16 = f32[8,128,512]{2,1,0:T(8,128)} copy(f32[8,128,512]{2,1,0:T(8,128)S(1)} %get-tuple-element.5) | data formatting | bytes 4194304
Async XLA Ops:
  2.2 1.6 %copy-start = (f32[8,128,512]{2,1,0:T(8,128)S(1)}, f32[8,128,512]{2,1,0:T(8,128)}, u32[]{:S(2)}) copy-start(f32[8,128,512]{2,1,0:T(8,128)} %substrate_hbm.1) | copy-start | bytes 6291460
  3.8 1.0 %copy-start.1 = (f32[1,1,256,512]{3,2,1,0:T(8,128)S(1)}, f32[1,1,256,512]{3,2,1,0:T(8,128)}, u32[]{:S(2)}) copy-start(f32[1,1,256,512]{3,2,1,0:T(8,128)} %param.16) | copy-start | bytes 1572868
  4.8 0.9 %copy-start.2 = (s32[128,512]{1,0:T(8,128)S(1)}, s32[128,512]{1,0:T(8,128)}, u32[]{:S(2)}) copy-start(s32[128,512]{1,0:T(8,128)} %kinds_hbm.1) | copy-start | bytes 786436
  5.8 0.9 %copy-start.3 = (f32[3,64,256]{2,1,0:T(8,128)S(1)}, f32[3,64,256]{2,1,0:T(8,128)}, u32[]{:S(2)}) copy-start(f32[3,64,256]{2,1,0:T(8,128)} %panels_ref.1) | copy-start | bytes 589828
  6.7 0.7 %copy-start.4 = (s32[1,128,1]{1,2,0:T(1,128)S(1)}, s32[1,128,1]{1,2,0:T(1,128)}, u32[]{:S(2)}) copy-start(s32[1,128,1]{1,2,0:T(1,128)} %param.12) | copy-start | bytes 1540
